TPU v7x, 256 devices: a whole 4x4x8 slice. The times are simulated.
256 devices in a mesh: row: 32 (over y, z), col: 8 (over x, core).
Axes of the slice: x: 4, y: 4, z: 8, core: 2. Of those that a mesh axis runs over, the one named last changes fastest.
Arguments:
- acts: bfloat16 [6144, 28672], P('col', 'row'), may hold values from -12 to 12
- out_grad: bfloat16 [6144, 8192], P('row', 'col'), may hold values from -12 to 12
- lengths: int32 [8], replicated, may hold values from 1 to 768, 4800 in all
Outputs:
- weight_grad: bfloat16 [28672, 8192], P('row', 'col')
- norms: float32 [8], replicated
All inputs are finite; a program needn't handle non-finite values.
Results may differ from a plain program's by a relative error of at most 0.0013.
Values may be sent and summed in bfloat16 or wider, within the bound.
No kernel may reach another device: no remote copies, remote signals or barrier semaphores. Data moves between devices by JAX's collectives and lax.ppermute only.
A program may use at most 128 MiB of HBM per device.

v0:
```python
import jax
import jax.numpy as jnp
from jax import lax
from jax.sharding import PartitionSpec as P

FF = 28672
D = 8192


def body(acts, out_grad, lengths):
    n_row = lax.axis_size("row")
    n_col = lax.axis_size("col")
    row_idx = lax.axis_index("row")
    col_idx = lax.axis_index("col")
    own_rows = out_grad.shape[0]
    tokens = own_rows * n_row
    seqs = lengths.shape[0]
    seq_len = tokens // seqs
    block = own_rows // n_col
    feats = acts.shape[1]
    width = out_grad.shape[1]
    positions = jnp.arange(tokens, dtype=jnp.int32)
    seq_of = positions // seq_len
    limit = jnp.sum(
        jnp.where(
            seq_of[:, None] == jnp.arange(seqs, dtype=jnp.int32)[None, :], lengths[None, :], 0
        ),
        axis=1,
    )
    live = positions % seq_len < limit
    act_full = lax.all_gather(acts, "col", axis=0, tiled=True)
    grad_full = lax.all_gather(out_grad, "row", axis=0, tiled=True)
    grads = jnp.where(live[:, None], grad_full, jnp.zeros_like(grad_full))
    act_seq = act_full.reshape(seqs, seq_len, feats)
    picked = lax.dynamic_index_in_dim(
        act_full.reshape(n_row, n_col, block, feats), col_idx, 1, keepdims=False
    )
    picked = picked.reshape(seqs, n_row // seqs * block, feats)
    act_part = jnp.einsum("sqf,slf->sql", picked, act_seq, preferred_element_type=jnp.float32)
    act_part = act_part.reshape(n_row * block, seq_len)
    summed = lax.psum(act_part.astype(jnp.bfloat16), "row").astype(jnp.float32)
    act_gram = lax.dynamic_slice_in_dim(summed, row_idx * block, block, 0)
    first = row_idx * own_rows
    own_seq = first // seq_len
    own_grads = lax.dynamic_slice_in_dim(grads, first, own_rows, 0)
    seq_grads = lax.dynamic_slice_in_dim(grads, own_seq * seq_len, seq_len, 0)
    grad_part = lax.dot_general(
        own_grads, seq_grads, (((1,), (1,)), ((), ())), preferred_element_type=jnp.float32
    )
    grad_gram = lax.psum_scatter(
        grad_part.astype(jnp.bfloat16), "col", scatter_dimension=0, tiled=True
    ).astype(jnp.float32)
    local = jnp.sum(act_gram * grad_gram)
    onehot = jnp.arange(seqs, dtype=jnp.int32) == own_seq
    squares = lax.psum(jnp.where(onehot, local, jnp.float32(0.0)), ("row", "col"))
    divisor = float(FF) * float(D) * float(seq_len)
    norms = jnp.sqrt(squares / divisor)
    scale = 1.0 / (norms + 0.1)
    total = jnp.zeros((feats, width), jnp.float32)
    for seq in range(seqs):
        act_rows = act_full[seq * seq_len : (seq + 1) * seq_len]
        grad_rows = grads[seq * seq_len : (seq + 1) * seq_len]
        product = lax.dot_general(
            act_rows, grad_rows, (((0,), (0,)), ((), ())), preferred_element_type=jnp.float32
        )
        total = total + scale[seq] * product
    weight_grad = (total / jnp.sqrt(jnp.float32(tokens))).astype(jnp.bfloat16)
    return (weight_grad, norms)


def solution(mesh):
    placed = (P("col", "row"), P("row", "col"), P())
    return jax.shard_map(
        body, mesh=mesh, in_specs=placed, out_specs=(P("row", "col"), P()), check_vma=False
    )
```

profile of v0, /device:TPU:1, one launch (start us, length us, event | category | flops | bytes accessed | tf_op | source)
XLA Modules:
  0.0 495.1 jit_solution(12963730170209471229)
XLA Ops:
  7.2 0.0 all-gather.3.cloned.1.call-start
  7.2 0.7 all-gather.3.cloned.1.call-update
  7.9 0.0 all-gather.5.cloned.1.call-start
  7.9 0.7 all-gather.5.cloned.1.call-update
  8.6 0.0 all-reduce.2.cloned.1.call-start
  8.7 0.8 select_reduce_fusion
  9.6 67.7 %all-gather.3.cloned.1.call-done = bf16[6144,896]{1,0:T(8,128)(2,1)} async-done(((bf16[768,896]{1,0:T(8,128)(2,1)}), bf16[6144,896]{1,0:T(8,128)(2,1)}) %all-gather.3.cloned.1.call-update) | async-done | bytes 11010064 | tf_op jit(solution)/shard_map/all_gather | solution.py:31
  77.2 1.5 constant_dynamic-slice_fusion
  78.7 8.6 %convolution_convert_fusion = bf16[8,96,768]{2,1,0:T(8,128)(2,1)} fusion(bf16[8,96,896]{2,1,0:T(8,128)(2,1)S(1)} %bitcast.20, bf16[8,768,896]{2,1,0:T(8,128)(2,1)} %bitcast.19), kind=kOutput, calls=%fused_computation.20 | convolution fusion | flops 1057554432 | bytes 13565952 | tf_op jit(solution)/shard_map/sqf,slf->sql/dot_general | solution.py:39
  87.3 0.0 all-reduce.2.cloned.1.call-update
  87.4 0.2 reduce-scatter.2.cloned.1.call-start
  87.6 110.4 %all-gather.5.cloned.1.call-done = bf16[6144,1024]{1,0:T(8,128)(2,1)} async-done(((bf16[192,1024]{1,0:T(8,128)(2,1)}), bf16[6144,1024]{1,0:T(8,128)(2,1)}) %all-gather.5.cloned.1.call-update) | async-done | bytes 12582928 | tf_op jit(solution)/shard_map/all_gather | solution.py:32
  197.9 6.4 %broadcast_select_fusion = bf16[6144,1024]{1,0:T(8,128)(2,1)S(1)} fusion(bf16[6144,1024]{1,0:T(8,128)(2,1)} %all-gather.5.cloned.1.call-done, pred[6144]{0:T(1024)(128)(4,1)S(1)} %fusion.32), kind=kLoop, calls=%fused_computation | loop fusion | flops 6291456 | bytes 25171968 | tf_op jit(solution)/shard_map/jit(_where)/select_n | solution.py:33
  204.3 4.5 copy-done
  208.9 1.4 fusion.28
  210.3 0.0 reduce-scatter.2.cloned.1.call-update
  210.3 5.7 %fusion.1 = f32[1024,896]{1,0:T(8,128)} fusion(bf16[6144,1024]{1,0:T(8,128)(2,1)} %copy-done, bf16[6144,896]{1,0:T(8,128)(2,1)} %all-gather.3.cloned.1.call-done), kind=kOutput, calls=%fused_computation.3 | convolution fusion | flops 1409286144 | bytes 6619136 | tf_op jit(solution)/shard_map/dot_general | solution.py:63
  216.0 5.7 %fusion.3 = f32[1024,896]{1,0:T(8,128)} fusion(bf16[6144,1024]{1,0:T(8,128)(2,1)} %copy-done, bf16[6144,896]{1,0:T(8,128)(2,1)} %all-gather.3.cloned.1.call-done), kind=kOutput, calls=%fused_computation.5 | convolution fusion | flops 1409286144 | bytes 6619136 | tf_op jit(solution)/shard_map/dot_general | solution.py:63
  221.7 5.0 %fusion.5 = f32[1024,896]{1,0:T(8,128)} fusion(bf16[6144,1024]{1,0:T(8,128)(2,1)S(1)} %copy-done.1, bf16[6144,896]{1,0:T(8,128)(2,1)} %all-gather.3.cloned.1.call-done), kind=kOutput, calls=%fused_computation.7 | convolution fusion | flops 1409286144 | bytes 6619136 | tf_op jit(solution)/shard_map/dot_general | solution.py:63
  226.7 5.1 %fusion.7 = f32[1024,896]{1,0:T(8,128)} fusion(bf16[6144,1024]{1,0:T(8,128)(2,1)S(1)} %copy-done.1, bf16[6144,896]{1,0:T(8,128)(2,1)} %all-gather.3.cloned.1.call-done), kind=kOutput, calls=%fused_computation.9 | convolution fusion | flops 1409286144 | bytes 6619136 | tf_op jit(solution)/shard_map/dot_general | solution.py:63
  231.9 5.0 %fusion.9 = f32[1024,896]{1,0:T(8,128)} fusion(bf16[6144,1024]{1,0:T(8,128)(2,1)S(1)} %copy-done.1, bf16[6144,896]{1,0:T(8,128)(2,1)} %all-gather.3.cloned.1.call-done), kind=kOutput, calls=%fused_computation.11 | convolution fusion | flops 1409286144 | bytes 6619136 | tf_op jit(solution)/shard_map/dot_general | solution.py:63
  236.9 5.0 %fusion.11 = f32[1024,896]{1,0:T(8,128)} fusion(bf16[6144,1024]{1,0:T(8,128)(2,1)S(1)} %copy-done.1, bf16[6144,896]{1,0:T(8,128)(2,1)} %all-gather.3.cloned.1.call-done), kind=kOutput, calls=%fused_computation.13 | convolution fusion | flops 1409286144 | bytes 6619136 | tf_op jit(solution)/shard_map/dot_general | solution.py:63
  241.8 103.9 %all-reduce.2.cloned.1.call-done = bf16[768,768]{1,0:T(8,128)(2,1)} async-done(((bf16[768,768]{1,0:T(8,128)(2,1)}), bf16[768,768]{1,0:T(8,128)(2,1)}) %all-reduce.2.cloned.1.call-update) | async-done | bytes 1179664 | tf_op jit(solution)/shard_map/psum | solution.py:41
  345.7 35.8 %reduce-scatter.2.cloned.1.call-done = bf16[24,768]{1,0:T(8,128)(2,1)} async-done(((bf16[192,768]{1,0:T(8,128)(2,1)}), bf16[24,768]{1,0:T(8,128)(2,1)}) %reduce-scatter.2.cloned.1.call-update) | async-done | bytes 36880 | tf_op jit(solution)/shard_map/reduce_scatter | solution.py:50
  381.5 1.4 multiply_reduce_fusion
  382.9 0.6 compare_select_fusion
  383.5 5.5 %fusion.13 = f32[1024,896]{1,0:T(8,128)} fusion(bf16[6144,1024]{1,0:T(8,128)(2,1)} %copy-done, bf16[6144,896]{1,0:T(8,128)(2,1)} %all-gather.3.cloned.1.call-done), kind=kOutput, calls=%fused_computation.15 | convolution fusion | flops 1409286144 | bytes 6619136 | tf_op jit(solution)/shard_map/dot_general | solution.py:63
  389.0 78.5 %psum.15 = f32[8]{0:T(128)S(1)} all-reduce(f32[8]{0:T(128)S(1)} %compare_select_fusion), channel_id=1, replica_groups=mesh['row'=32,'col'=8] {'row','col'}, use_global_device_ids=true, to_apply=%region_4.5 | all-reduce | flops 8 | bytes 64 | tf_op jit(solution)/shard_map/psum | solution.py:55
  467.5 0.5 add_divide_fusion
  468.0 0.6 fusion.39
  468.6 17.5 %fusion.17 = bf16[896,1024]{0,1:T(8,128)(2,1)S(1)} fusion(bf16[6144,1024]{1,0:T(8,128)(2,1)} %copy-done, f32[]{:T(128)} %bitcast.11, f32[1024,896]{1,0:T(8,128)} %fusion.1, f32[]{:T(128)} %bitcast.10, f32[1024,896]{1,0:T(8,128)} %fusion.3, f32[]{:T(128)} %bitcast.9, f32[1024,896]{1,0:T(8,128)} %fusion.5, f32[]{:T(128)} %bitcast.8, f32[1024,896]{1,0:T(8,128)} %fusion.7, ...), kind=kOutput, calls=%fused_computation.19 | convolution fusion | flops 1424883712 | bytes 30478336 | tf_op jit(solution)/shard_map/dot_general | solution.py:63
  486.1 2.4 copy.8
  (5 shorter events, 0.0 us)
Async XLA Ops:
  7.2 70.1 %all-gather.3.cloned.1.call-start = ((), (), s32[]{:S(2)}) async-start(), calls=%async_computation.1 | async-start | bytes 12386304 | tf_op jit(solution)/shard_map/all_gather | solution.py:31
  7.9 190.0 %all-gather.5.cloned.1.call-start = ((), (), s32[]{:S(2)}) async-start(), calls=%async_computation.3 | async-start | bytes 12976128 | tf_op jit(solution)/shard_map/all_gather | solution.py:32
  8.6 337.1 %all-reduce.2.cloned.1.call-start = ((), (), s32[]{:S(2)}) async-start(), calls=%async_computation.2 | async-start | bytes 2359296 | tf_op jit(solution)/shard_map/psum | solution.py:41
  87.4 294.1 %reduce-scatter.2.cloned.1.call-start = ((), (), s32[]{:S(2)}) async-start(), calls=%async_computation.4 | async-start | bytes 331776 | tf_op jit(solution)/shard_map/reduce_scatter | solution.py:50
  204.3 4.6 copy-start
  210.3 11.4 %copy-start.1 = (bf16[6144,1024]{1,0:T(8,128)(2,1)S(1)}, bf16[6144,1024]{1,0:T(8,128)(2,1)}, u32[]{:S(2)}) copy-start(bf16[6144,1024]{1,0:T(8,128)(2,1)} %copy-done) | copy-start | bytes 37748740
Sparse Core Ops, SparseCore 0:
  9.8 67.3 all-gather.2
  79.8 118.0 all-gather.4
  201.9 143.7 all-reduce.1
  348.1 33.3 reduce-scatter.1
where the time goes:
time: 496 us; the launch traced here: 495 us
  waiting for transfers between devices  319 us (64%)
  blocking collectives  78.5 us (16%)
  matrix products  64.5 us (13%)
  between operations  13.9 us (3%)
  other arithmetic  9.76 us (2%)
  local copies, waits for them, and re-layouts  9.06 us (2%)
    all_gather x1, waiting for transfers between devices, body(): grad_full = lax.all_gather(out_grad, 'row', axis=0, tiled=True)  110 us
    psum x1, waiting for transfers between devices, body(): summed = lax.psum(act_part.astype(jnp.bfloat16), 'row').astype(jnp.float32)  104 us
    psum x1, blocking collectives, body(): lax.psum(jnp.where(onehot, local, jnp.float32(0.0)), ('row', 'col'))  78.5 us
    all_gather x1, waiting for transfers between devices, body(): act_full = lax.all_gather(acts, 'col', axis=0, tiled=True)  67.7 us
    dot_general x8, matrix products, body(): lax.dot_general(act_rows, grad_rows, (((0,), (0,)), ((), ())), preferred_...  54.5 us
    reduce_scatter x1, waiting for transfers between devices, body(): lax.psum_scatter(grad_part.astype(jnp.bfloat16), 'col', scatter_dimension...  35.8 us
  transfers between devices with their start and end apart: 4, of which 4 were waited for; matrix products, arithmetic and copies ran while one was open for 10% of the time, Pallas kernels for 0%

commit v1 on v0

v1 whole, which is shorter than its diff:
```python
import jax
import jax.numpy as jnp
from jax import lax
from jax.sharding import PartitionSpec as P

FF = 28672
D = 8192


def exchange_sum(value, axis, shifts):
    size = lax.axis_size(axis)
    parts = [value]
    for shift in shifts:
        parts.append(lax.ppermute(value, axis, [(i, i ^ shift) for i in range(size)]))
    while len(parts) > 1:
        parts = [parts[i] + parts[i + 1] for i in range(0, len(parts), 2)]
    return parts[0]


def sum_everywhere(value):
    value = exchange_sum(value, "col", (1,))
    value = exchange_sum(value, "col", (2, 4, 6))
    value = exchange_sum(value, "row", (8, 16, 24))
    value = exchange_sum(value, "row", (1, 2, 3))
    return exchange_sum(value, "row", (4,))


def body(acts, out_grad, lengths):
    n_row = lax.axis_size("row")
    row_idx = lax.axis_index("row")
    own_rows = out_grad.shape[0]
    tokens = own_rows * n_row
    seqs = lengths.shape[0]
    seq_len = tokens // seqs
    positions = row_idx * own_rows + jnp.arange(own_rows, dtype=jnp.int32)
    seq_of = positions // seq_len
    limit = jnp.sum(
        jnp.where(
            seq_of[:, None] == jnp.arange(seqs, dtype=jnp.int32)[None, :], lengths[None, :], 0
        ),
        axis=1,
    )
    live = positions % seq_len < limit
    own_grads = jnp.where(live[:, None], out_grad, jnp.zeros_like(out_grad))
    grads = lax.all_gather(own_grads, "row", axis=0, tiled=True)
    act_full = lax.all_gather(acts, "col", axis=0, tiled=True)
    products = []
    sums = []
    for seq in range(seqs):
        act_rows = act_full[seq * seq_len : (seq + 1) * seq_len]
        grad_rows = grads[seq * seq_len : (seq + 1) * seq_len]
        product = lax.dot_general(
            act_rows, grad_rows, (((0,), (0,)), ((), ())), preferred_element_type=jnp.float32
        )
        products.append(product)
        sums.append(jnp.sum(product * product))
    squares = sum_everywhere(jnp.stack(sums))
    norms = jnp.sqrt(squares / (float(FF) * float(D) * float(seq_len)))
    scale = 1.0 / (norms + 0.1)
    total = scale[0] * products[0]
    for seq in range(1, seqs):
        total = total + scale[seq] * products[seq]
    weight_grad = (total / jnp.sqrt(jnp.float32(tokens))).astype(jnp.bfloat16)
    return (weight_grad, norms)


def solution(mesh):
    placed = (P("col", "row"), P("row", "col"), P())
    return jax.shard_map(
        body, mesh=mesh, in_specs=placed, out_specs=(P("row", "col"), P()), check_vma=False
    )
```

time: 496 us -> 299 us (0.60)
  waiting for transfers between devices: 319 us -> 201 us
  blocking collectives: 78.5 us -> 0 us
  matrix products: 64.5 us -> 39.5 us
  starting transfers between devices: 0.34 us -> 13.2 us
  other arithmetic: 9.76 us -> 18.6 us
    psum x1 -> x0, waiting for transfers between devices: 104 us -> none  [body(): summed = lax.psum(act_part.astype(jnp.bfloat16), 'row').astype(jnp.float32)]
    psum x1 -> x0, blocking collectives: 78.5 us -> none  [body(): lax.psum(jnp.where(onehot, local, jnp.float32(0.0)), ('row', 'col'))]
    reduce_scatter x1 -> x0, waiting for transfers between devices: 35.8 us -> none  [body(): lax.psum_scatter(grad_part.astype(jnp.bfloat16), 'col', scatter_dimension...]
    convert_element_type x0 -> x1, other arithmetic: none -> 15.5 us  [body(): weight_grad = (total / jnp.sqrt(jnp.float32(tokens))).astype(jnp.bfloat16)]
    dot_general x8, matrix products: 54.5 us -> 39.5 us  [body(): lax.dot_general(act_rows, grad_rows, (((0,), (0,)), ((), ())), preferred_...]
    ppermute x0 -> x11, starting transfers between devices: none -> 13.1 us  [exchange_sum(): lax.ppermute(value, axis, [(i, i ^ shift) for i in range(size)])]
    ppermute x0 -> x11, waiting for transfers between devices: none -> 12.6 us  [exchange_sum(): lax.ppermute(value, axis, [(i, i ^ shift) for i in range(size)])]
    all_gather x1, waiting for transfers between devices: 110 us -> 121 us  [body(): grads = lax.all_gather(own_grads, 'row', axis=0, tiled=True)]
  transfers between devices with their start and end apart: 4 -> 13, of which waited for: 4 -> 10; matrix products, arithmetic and copies ran while one was open for 10% -> 1% of each run, Pallas kernels for 0% -> 0%
where the time goes in v1:
time: 299 us; the launch traced here: 295 us
  waiting for transfers between devices  201 us (67%)
  matrix products  39.5 us (13%)
  other arithmetic  18.6 us (6%)
  between operations  14.1 us (5%)
  starting transfers between devices  13.2 us (4%)
  local copies, waits for them, and re-layouts  8.23 us (3%)
    all_gather x1, waiting for transfers between devices, body(): grads = lax.all_gather(own_grads, 'row', axis=0, tiled=True)  121 us
    all_gather x1, waiting for transfers between devices, body(): act_full = lax.all_gather(acts, 'col', axis=0, tiled=True)  66.6 us
    dot_general x8, matrix products, body(): lax.dot_general(act_rows, grad_rows, (((0,), (0,)), ((), ())), preferred_...  39.5 us
    convert_element_type x1, other arithmetic, body(): weight_grad = (total / jnp.sqrt(jnp.float32(tokens))).astype(jnp.bfloat16)  15.5 us
    ppermute x11, starting transfers between devices, exchange_sum(): lax.ppermute(value, axis, [(i, i ^ shift) for i in range(size)])  13.1 us
    ppermute x11, waiting for transfers between devices, exchange_sum(): lax.ppermute(value, axis, [(i, i ^ shift) for i in range(size)])  12.6 us
  transfers between devices with their start and end apart: 13, of which 10 were waited for; matrix products, arithmetic and copies ran while one was open for 1% of the time, Pallas kernels for 0%

profile of v1, /device:TPU:1, one launch (start us, length us, event | category | flops | bytes accessed | tf_op | source)
XLA Modules:
  0.0 294.8 jit_solution(15958608026676265516)
XLA Ops:
  7.2 0.7 all-gather.5.cloned.1.call-update
  8.0 0.7 select_reduce_fusion
  8.7 1.8 broadcast_select_fusion
  10.6 66.6 %all-gather.5.cloned.1.call-done = bf16[6144,896]{1,0:T(8,128)(2,1)} async-done(((bf16[768,896]{1,0:T(8,128)(2,1)}), bf16[6144,896]{1,0:T(8,128)(2,1)}) %all-gather.5.cloned.1.call-update) | async-done | bytes 11010064 | tf_op jit(solution)/shard_map/all_gather | solution.py:46
  77.2 121.3 %all-gather.3.cloned.1.call-done = bf16[6144,1024]{1,0:T(8,128)(2,1)} async-done(((bf16[192,1024]{1,0:T(8,128)(2,1)}), bf16[6144,1024]{1,0:T(8,128)(2,1)}) %all-gather.3.cloned.1.call-update) | async-done | bytes 12582928 | tf_op jit(solution)/shard_map/all_gather | solution.py:45
  198.5 6.3 %multiply_reduce_fusion = (f32[]{:T(128)}, f32[1024,896]{1,0:T(8,128)}) fusion(bf16[6144,896]{1,0:T(8,128)(2,1)} %all-gather.5.cloned.1.call-done, bf16[6144,1024]{1,0:T(8,128)(2,1)} %all-gather.3.cloned.1.call-done), kind=kOutput, calls=%fused_computation.1 | convolution fusion | flops 1411121152 | bytes 6619140 | tf_op jit(solution)/shard_map/dot_general | solution.py:52
  204.8 7.0 %multiply_reduce_fusion.1 = (f32[]{:T(128)}, f32[1024,896]{1,0:T(8,128)}) fusion(bf16[6144,896]{1,0:T(8,128)(2,1)} %all-gather.5.cloned.1.call-done, bf16[6144,1024]{1,0:T(8,128)(2,1)} %all-gather.3.cloned.1.call-done), kind=kOutput, calls=%fused_computation.2 | convolution fusion | flops 1411121152 | bytes 6619140 | tf_op jit(solution)/shard_map/dot_general | solution.py:52
  211.8 4.3 %multiply_reduce_fusion.2 = (f32[]{:T(128)}, f32[1024,896]{1,0:T(8,128)}) fusion(bf16[6144,896]{1,0:T(8,128)(2,1)S(1)} %copy-done, bf16[6144,1024]{1,0:T(8,128)(2,1)S(1)} %bitcast.19), kind=kOutput, calls=%fused_computation.3 | convolution fusion | flops 1411121152 | bytes 6619140 | tf_op jit(solution)/shard_map/dot_general | solution.py:52
  216.2 4.3 %multiply_reduce_fusion.3 = (f32[]{:T(128)}, f32[1024,896]{1,0:T(8,128)}) fusion(bf16[6144,896]{1,0:T(8,128)(2,1)S(1)} %copy-done, bf16[6144,1024]{1,0:T(8,128)(2,1)S(1)} %bitcast.19), kind=kOutput, calls=%fused_computation.4 | convolution fusion | flops 1411121152 | bytes 6619140 | tf_op jit(solution)/shard_map/dot_general | solution.py:52
  220.4 4.4 %multiply_reduce_fusion.4 = (f32[]{:T(128)}, f32[1024,896]{1,0:T(8,128)}) fusion(bf16[6144,896]{1,0:T(8,128)(2,1)S(1)} %copy-done, bf16[6144,1024]{1,0:T(8,128)(2,1)S(1)} %bitcast.19), kind=kOutput, calls=%fused_computation.5 | convolution fusion | flops 1411121152 | bytes 6619140 | tf_op jit(solution)/shard_map/dot_general | solution.py:52
  224.9 4.4 %multiply_reduce_fusion.5 = (f32[]{:T(128)}, f32[1024,896]{1,0:T(8,128)}) fusion(bf16[6144,896]{1,0:T(8,128)(2,1)S(1)} %copy-done, bf16[6144,1024]{1,0:T(8,128)(2,1)S(1)} %bitcast.19), kind=kOutput, calls=%fused_computation.6 | convolution fusion | flops 1411121152 | bytes 6619140 | tf_op jit(solution)/shard_map/dot_general | solution.py:52
  229.2 4.5 %multiply_reduce_fusion.6 = (f32[]{:T(128)}, f32[1024,896]{1,0:T(8,128)}) fusion(bf16[6144,896]{1,0:T(8,128)(2,1)S(1)} %copy-done, bf16[6144,1024]{1,0:T(8,128)(2,1)S(1)} %bitcast.19), kind=kOutput, calls=%fused_computation.7 | convolution fusion | flops 1411121152 | bytes 6619140 | tf_op jit(solution)/shard_map/dot_general | solution.py:52
  233.8 4.2 %multiply_reduce_fusion.7 = (f32[]{:T(128)}, f32[1024,896]{1,0:T(8,128)}) fusion(bf16[6144,896]{1,0:T(8,128)(2,1)S(1)} %copy-done, bf16[6144,1024]{1,0:T(8,128)(2,1)S(1)} %bitcast.19), kind=kOutput, calls=%fused_computation.8 | convolution fusion | flops 1411121152 | bytes 6619140 | tf_op jit(solution)/shard_map/dot_general | solution.py:52
  238.0 5.1 %stack.35 = f32[8]{0:T(128)S(1)} concatenate(f32[1]{0:T(128)} %bitcast, f32[1]{0:T(128)} %bitcast.1, f32[1]{0:T(128)} %bitcast.2, f32[1]{0:T(128)} %bitcast.3, f32[1]{0:T(128)} %bitcast.4, f32[1]{0:T(128)} %bitcast.5, f32[1]{0:T(128)} %bitcast.6, f32[1]{0:T(128)} %bitcast.7), dimensions={0} | concatenate | bytes 64 | tf_op jit(solution)/shard_map/stack | solution.py:57
  243.2 1.4 collective-permute-start
  244.6 0.8 collective-permute-done
  245.4 2.4 collective-permute-start.3
  247.8 0.6 collective-permute-start.2
  249.0 2.7 collective-permute-done.2
  251.8 0.6 collective-permute-start.6
  252.4 1.2 collective-permute-start.5
  253.6 1.5 collective-permute-start.4
  255.5 0.8 collective-permute-done.5
  256.3 2.8 collective-permute-start.9
  259.1 0.8 collective-permute-start.7
  260.0 0.7 collective-permute-done.9
  260.6 1.8 collective-permute-done.8
  262.5 1.5 collective-permute-start.10
  263.9 5.0 %collective-permute-done.10 = f32[8]{0:T(128)S(1)} collective-permute-done((f32[8]{0:T(128)S(1)}, f32[8]{0:T(128)S(1)}, u32[]{:S(2)}, u32[]{:S(2)}) %collective-permute-start.10) | collective-permute-done | bytes 64 | tf_op jit(solution)/shard_map/ppermute | solution.py:14
  269.4 0.7 fusion.28
  270.1 15.5 %fusion = bf16[896,1024]{0,1:T(8,128)(2,1)S(1)} fusion(f32[1024,896]{1,0:T(8,128)} %get-tuple-element.31, f32[]{:T(128)} %bitcast.15, f32[1024,896]{1,0:T(8,128)} %get-tuple-element.29, f32[]{:T(128)} %bitcast.14, f32[1024,896]{1,0:T(8,128)} %get-tuple-element.27, f32[]{:T(128)} %bitcast.13, f32[1024,896]{1,0:T(8,128)} %get-tuple-element.25, f32[]{:T(128)} %bitcast.12, ...), kind=kLoop, calls=%fused_computation.9 | loop fusion | flops 15597568 | bytes 31195168 | tf_op jit(solution)/shard_map/convert_element_type | solution.py:63
  285.5 2.4 copy.6
  (26 shorter events, 1.7 us)
Async XLA Ops:
  7.2 70.1 %all-gather.5.cloned.1.call-start = ((), (), s32[]{:S(2)}) async-start(), calls=%async_computation.1 | async-start | bytes 12386304 | tf_op jit(solution)/shard_map/all_gather | solution.py:46
  7.9 190.6 %all-gather.3.cloned.1.call-start = ((), (), s32[]{:S(2)}) async-start(), calls=%async_computation | async-start | bytes 12976128 | tf_op jit(solution)/shard_map/all_gather | solution.py:45
  198.5 13.3 %slice-start = ((s8[12582912]{0:T(1024)(128)(4,1)}), s8[4194304]{0:T(1024)(128)(4,1)S(1)}, s32[]{:S(2)}) async-start(s8[12582912]{0:T(1024)(128)(4,1)} %bitcast.18), calls=%async_computation.2 | async-start | bytes 8388608
  198.5 13.3 %slice-start.1 = ((s8[12582912]{0:T(1024)(128)(4,1)}), s8[4194304]{0:T(1024)(128)(4,1)S(1)}, s32[]{:S(2)}) async-start(s8[12582912]{0:T(1024)(128)(4,1)} %bitcast.18), calls=%async_computation.3 | async-start | bytes 8388608
  198.5 13.3 %copy-start = (bf16[6144,896]{1,0:T(8,128)(2,1)S(1)}, bf16[6144,896]{1,0:T(8,128)(2,1)}, u32[]{:S(2)}) copy-start(bf16[6144,896]{1,0:T(8,128)(2,1)} %all-gather.5.cloned.1.call-done) | copy-start | bytes 33030148
  204.8 7.1 %slice-start.2 = ((s8[12582912]{0:T(1024)(128)(4,1)}), s8[4194304]{0:T(1024)(128)(4,1)S(1)}, s32[]{:S(2)}) async-start(s8[12582912]{0:T(1024)(128)(4,1)} %bitcast.18), calls=%async_computation.4 | async-start | bytes 8388608
  243.2 2.3 collective-permute-start
  245.4 3.6 %collective-permute-start.3 = (f32[8]{0:T(128)S(1)}, f32[8]{0:T(128)S(1)}, u32[]{:S(2)}, u32[]{:S(2)}) collective-permute-start(f32[8]{0:T(128)S(1)} %add.93), channel_id=1, source_target_pairs={{0,6},{1,7},{2,4},{3,5},{4,2},{5,3},{6,0},{7,1},{8,14},{9,15},{10,... | collective-permute-start | bytes 104 | tf_op jit(solution)/shard_map/ppermute | solution.py:14
  247.8 3.9 %collective-permute-start.2 = (f32[8]{0:T(128)S(1)}, f32[8]{0:T(128)S(1)}, u32[]{:S(2)}, u32[]{:S(2)}) collective-permute-start(f32[8]{0:T(128)S(1)} %add.93), channel_id=1, source_target_pairs={{0,4},{1,5},{2,6},{3,7},{4,0},{5,1},{6,2},{7,3},{8,12},{9,13},{10,... | collective-permute-start | bytes 104 | tf_op jit(solution)/shard_map/ppermute | solution.py:14
  248.4 3.4 %collective-permute-start.1 = (f32[8]{0:T(128)S(1)}, f32[8]{0:T(128)S(1)}, u32[]{:S(2)}, u32[]{:S(2)}) collective-permute-start(f32[8]{0:T(128)S(1)} %add.93), channel_id=1, source_target_pairs={{0,2},{1,3},{2,0},{3,1},{4,6},{5,7},{6,4},{7,5},{8,10},{9,11},{10,... | collective-permute-start | bytes 104 | tf_op jit(solution)/shard_map/ppermute | solution.py:14
  251.8 3.7 %collective-permute-start.6 = (f32[8]{0:T(128)S(1)}, f32[8]{0:T(128)S(1)}, u32[]{:S(2)}, u32[]{:S(2)}) collective-permute-start(f32[8]{0:T(128)S(1)} %add_add_fusion.2), channel_id=1, source_target_pairs={{0,192},{8,200},{16,208},{24,216},{32,224},{40,232},{48,240},{56,2... | collective-permute-start | bytes 104 | tf_op jit(solution)/shard_map/ppermute | solution.py:14
  252.4 3.9 %collective-permute-start.5 = (f32[8]{0:T(128)S(1)}, f32[8]{0:T(128)S(1)}, u32[]{:S(2)}, u32[]{:S(2)}) collective-permute-start(f32[8]{0:T(128)S(1)} %add_add_fusion.2), channel_id=1, source_target_pairs={{0,128},{8,136},{16,144},{24,152},{32,160},{40,168},{48,176},{56,1... | collective-permute-start | bytes 104 | tf_op jit(solution)/shard_map/ppermute | solution.py:14
  253.6 2.8 collective-permute-start.4
  256.3 4.3 %collective-permute-start.9 = (f32[8]{0:T(128)S(1)}, f32[8]{0:T(128)S(1)}, u32[]{:S(2)}, u32[]{:S(2)}) collective-permute-start(f32[8]{0:T(128)S(1)} %add_add_fusion.1), channel_id=1, source_target_pairs={{0,24},{8,16},{16,8},{24,0},{32,56},{40,48},{48,40},{56,32},{64,88... | collective-permute-start | bytes 104 | tf_op jit(solution)/shard_map/ppermute | solution.py:14
  259.1 3.3 %collective-permute-start.8 = (f32[8]{0:T(128)S(1)}, f32[8]{0:T(128)S(1)}, u32[]{:S(2)}, u32[]{:S(2)}) collective-permute-start(f32[8]{0:T(128)S(1)} %add_add_fusion.1), channel_id=1, source_target_pairs={{0,16},{8,24},{16,0},{24,8},{32,48},{40,56},{48,32},{56,40},{64,80... | collective-permute-start | bytes 104 | tf_op jit(solution)/shard_map/ppermute | solution.py:14
  259.1 3.3 %collective-permute-start.7 = (f32[8]{0:T(128)S(1)}, f32[8]{0:T(128)S(1)}, u32[]{:S(2)}, u32[]{:S(2)}) collective-permute-start(f32[8]{0:T(128)S(1)} %add_add_fusion.1), channel_id=1, source_target_pairs={{0,8},{8,0},{16,24},{24,16},{32,40},{40,32},{48,56},{56,48},{64,72... | collective-permute-start | bytes 104 | tf_op jit(solution)/shard_map/ppermute | solution.py:14
  262.5 6.4 %collective-permute-start.10 = (f32[8]{0:T(128)S(1)}, f32[8]{0:T(128)S(1)}, u32[]{:S(2)}, u32[]{:S(2)}) collective-permute-start(f32[8]{0:T(128)S(1)} %add_add_fusion), channel_id=1, source_target_pairs={{0,32},{8,40},{16,48},{24,56},{32,0},{40,8},{48,16},{56,24},{64,96... | collective-permute-start | bytes 104 | tf_op jit(solution)/shard_map/ppermute | solution.py:14
Sparse Core Ops, SparseCore 0:
  9.8 67.3 all-gather.4
  80.4 118.0 all-gather.2
